TPU v7x, 128 devices: a whole 4x4x4 slice. The times are simulated.
128 devices in a mesh: song: 2 (over y_lo), seq: 64 (over z, x, y_hi, core).
Axes of the slice: x: 4, y: 4 (y_hi: 2, y_lo: 2; y = y_hi * 2 + y_lo), z: 4, core: 2. Of those that a mesh axis runs over, the one named last changes fastest.
Arguments:
- song_ids: int32 [16384], P(('song', 'seq')), parts along dimension 0, may hold values from 0 to 2047
- table: bfloat16 [2048, 2432], P(None, 'seq'), may hold values from -6 to 6
- position_table: bfloat16 [8192, 2432], P('seq'), may hold values from -4 to 4
- w_qkv: bfloat16 [2, 2432, 1800], replicated, may hold values from -4 to 4
- w_out: bfloat16 [2, 600, 2432], replicated, may hold values from -0.25 to 0.25
Outputs:
- stream_out: bfloat16 [16384, 2432], P(('song', 'seq')), parts along dimension 0
There are 2 independent parts, one for each index of `song`. A program takes and returns all parts, laid end to end along the dimension named above; an argument that names none is the same for every part. Nothing has to cross between parts.
All inputs are finite; a program needn't handle non-finite values.
Results may differ from a plain program's by a relative error of at most 0.0065.
Values may be sent and summed in bfloat16 or wider, within the bound.
No kernel may reach another device: no remote copies, remote signals or barrier semaphores. Data moves between devices by JAX's collectives and lax.ppermute only.
A program may use at most 192 MiB of HBM per device.

v0:
```python
import math
import jax
import jax.numpy as jnp
from jax import lax
from jax.sharding import PartitionSpec as P

HEADS = 4
HEAD = 150
epsilon = 1e-05


def from_behind(value, axis, by):
    length = lax.axis_size(axis)
    pairs = [(i, i + by) for i in range(length) if 0 <= i + by < length]
    return lax.ppermute(value, axis, pairs)


def normalize(residual):
    center_mean = jnp.mean(residual, axis=-1, keepdims=True)
    centered = residual - center_mean
    variance = jnp.mean(centered * centered, axis=-1, keepdims=True)
    return (centered * lax.rsqrt(variance + epsilon)).astype(jnp.bfloat16)


def project(residual, weight):
    joined = jnp.dot(normalize(residual), weight, preferred_element_type=jnp.float32).astype(
        jnp.bfloat16
    )
    return joined.reshape(residual.shape[0], HEADS, 3 * HEAD)


def softmax_rounded(scores):
    top_score = jnp.max(scores, axis=-1, keepdims=True)
    lifted = jnp.exp(scores - top_score)
    return (lifted / jnp.sum(lifted, axis=-1, keepdims=True)).astype(jnp.bfloat16)


def shards(song_ids, table, position_table, w_qkv, w_out):
    inv_root = 1.0 / math.sqrt(HEAD)
    axis_count = lax.axis_size("seq")
    row_index = lax.axis_index("seq")
    all_codes = lax.all_gather(song_ids, "seq", axis=0, tiled=True)
    picked = jnp.take(table, all_codes, axis=0)
    embedded = lax.all_to_all(picked, "seq", split_axis=0, concat_axis=1, tiled=True)
    residual = embedded.astype(jnp.float32) + position_table.astype(jnp.float32)
    local_tokens = residual.shape[0]
    joined = project(residual, w_qkv[0])
    every_row = lax.all_gather(joined[:, :, HEAD:], "seq", axis=0, tiled=True)
    row_grid = every_row.reshape(axis_count, local_tokens, HEADS, 2 * HEAD)
    scores = (
        jnp.einsum(
            "chd,rchd->chr",
            joined[:, :, :HEAD],
            row_grid[..., :HEAD],
            preferred_element_type=jnp.float32,
        )
        * inv_root
    )
    allowed = jnp.arange(axis_count) <= row_index
    probs = softmax_rounded(jnp.where(allowed, scores, -jnp.inf))
    mixed = jnp.einsum(
        "chr,rchd->chd", probs, row_grid[..., HEAD:], preferred_element_type=jnp.float32
    ).astype(jnp.bfloat16)
    residual = residual + jnp.dot(
        mixed.reshape(local_tokens, HEADS * HEAD), w_out[0], preferred_element_type=jnp.float32
    )
    joined = project(residual, w_qkv[1])
    before = from_behind(joined[:, :, HEAD:], "seq", 1)
    query = joined[:, :, :HEAD]
    far_scores = (
        jnp.einsum("chd,khd->hck", query, before[..., :HEAD], preferred_element_type=jnp.float32)
        * inv_root
    )
    far_scores = jnp.where(row_index > 0, far_scores, -jnp.inf)
    own_scores = (
        jnp.einsum(
            "chd,chd->hc", query, joined[:, :, HEAD : 2 * HEAD], preferred_element_type=jnp.float32
        )
        * inv_root
    )
    top_score = jnp.maximum(jnp.max(far_scores, axis=-1), own_scores)
    far_lifted = jnp.exp(far_scores - top_score[..., None])
    own_lifted = jnp.exp(own_scores - top_score)
    total = jnp.sum(far_lifted, axis=-1) + own_lifted
    far_probs = (far_lifted / total[..., None]).astype(jnp.bfloat16)
    own_probs = (own_lifted / total).astype(jnp.bfloat16)
    far_part = jnp.einsum(
        "hck,khd->chd", far_probs, before[..., HEAD:], preferred_element_type=jnp.float32
    )
    own_part = jnp.transpose(own_probs.astype(jnp.float32))[..., None] * joined[
        :, :, 2 * HEAD :
    ].astype(jnp.float32)
    mixed = (far_part + own_part).astype(jnp.bfloat16)
    residual = residual + jnp.dot(
        mixed.reshape(local_tokens, HEADS * HEAD), w_out[1], preferred_element_type=jnp.float32
    )
    return residual.astype(jnp.bfloat16)


def solution(mesh):
    in_specs = (P(("song", "seq")), P(None, "seq"), P("seq", None), P(), P())
    out_specs = P(("song", "seq"), None)
    return jax.shard_map(shards, mesh=mesh, in_specs=in_specs, out_specs=out_specs, check_vma=False)
```

profile of v0, /device:TPU:32, one launch (start us, length us, event | category | flops | bytes accessed | tf_op | source)
XLA Modules:
  0.0 349.5 jit_solution(981527527557596328)
XLA Ops:
  6.5 0.0 all-gather.3.cloned.1.call-start
  6.5 83.1 %all-gather = s32[64,1,128]{2,1,0:T(1,128)S(1)} all-gather(s32[1,1,128]{2,1,0:T(1,128)} %bitcast.80), channel_id=1, replica_groups=mesh['song'=2,'seq'=64] {'seq'}, dimensions={0}, use_global_device_ids=true | all-gather | bytes 33280 | tf_op jit(solution)/shard_map/all_gather | solution.py:42
  89.7 1.2 copy.17
  90.9 24.0 %gather_fusion = bf16[8192,38]{1,0:T(8,128)(2,1)S(1)} fusion(bf16[2048,38]{1,0:T(8,128)(2,1)S(1)} %copy.17, s32[8192]{0:T(1024)S(1)} %fusion.43), kind=kCustom, calls=%fused_computation | custom fusion | bytes 1277952 | tf_op jit(solution)/shard_map/jit(_take)/gather | solution.py:43
  115.0 1.0 copy.18
  116.0 0.1 broadcast_select_fusion
  116.1 31.4 %all_to_all.10 = bf16[64,128,38]{1,2,0:T(8,128)(2,1)S(1)} all-to-all(bf16[64,128,38]{1,2,0:T(8,128)(2,1)S(1)} %broadcast_select_fusion), channel_id=1, replica_groups=mesh['song'=2,'seq'=64] {'seq'}, dimensions={0} | all-to-all | bytes 1245184 | tf_op jit(solution)/shard_map/all_to_all | solution.py:44
  147.5 0.1 convert_bitcast_fusion
  147.6 0.1 reshape.65
  147.7 0.0 copy-start
  147.7 0.4 copy.19
  148.1 0.7 copy-done
  148.7 0.2 fusion.39
  149.0 0.3 multiply_reduce_fusion.3
  149.3 6.2 %fusion.13 = bf16[128,1800]{0,1:T(8,128)(2,1)S(1)} fusion(bf16[2,2432,1800]{1,2,0:T(8,128)(2,1)} %param.8, f32[128]{0:T(128)S(1)} %add_rsqrt_fusion.1, f32[128]{0:T(128)S(1)} %broadcast_multiply_fusion.1, f32[128,2432]{1,0:T(8,128)S(1)} %copy.19, bf16[128,2432]{1,0:T(8,128)(2,1)S(1)} %copy-done), kind=kOutput, calls=%fused_computation.20 | convolution fusion | flops 1122452480 | bytes 11084800 | tf_op jit(solution)/shard_map/dot_general | solution.py:26
  155.5 0.1 reshape.60
  155.6 0.8 slice.59
  156.4 0.0 all-gather.3.cloned.1.call-update
  156.5 117.3 %all-gather.3.cloned.1.call-done = bf16[8192,4,300]{0,2,1:T(8,128)(2,1)} async-done(((bf16[128,4,300]{0,2,1:T(8,128)(2,1)}), bf16[8192,4,300]{0,2,1:T(8,128)(2,1)}) %all-gather.3.cloned.1.call-update) | async-done | bytes 19660816 | tf_op jit(solution)/shard_map/all_gather | solution.py:48
  273.8 27.6 %reshape.61 = bf16[64,128,4,300]{1,0,3,2:T(8,128)(2,1)} reshape(bf16[8192,4,300]{0,2,1:T(8,128)(2,1)} %all-gather.3.cloned.1.call-done) | data formatting | bytes 39321600 | tf_op jit(solution)/shard_map/reshape | solution.py:49
  301.3 6.7 %multiply_reduce_fusion.1 = f32[128,4,64]{0,2,1:T(8,128)S(1)} fusion(bf16[64,128,4,300]{1,0,3,2:T(8,128)(2,1)} %reshape.61, f32[128,4,150]{0,2,1:T(8,128)S(1)} %slice_convert_fusion), kind=kLoop, calls=%fused_computation.4 | loop fusion | flops 14712832 | bytes 10268672 | tf_op jit(solution)/shard_map/chd,rchd->chr/dot_general | solution.py:51
  308.0 0.1 fusion.26
  308.2 8.3 %multiply_reduce_fusion = bf16[128,4,150]{0,2,1:T(8,128)(2,1)S(1)} fusion(bf16[64,128,4,300]{1,0,3,2:T(8,128)(2,1)} %reshape.61, f32[128,4,64]{0,2,1:T(8,128)S(1)} %fusion.26), kind=kLoop, calls=%fused_computation.3 | loop fusion | flops 14668800 | bytes 10115072 | tf_op jit(solution)/shard_map/chr,rchd->chd/dot_general | solution.py:61
  316.6 2.6 fusion.53
  319.2 0.3 multiply_reduce_fusion.2
  319.5 6.2 %fusion.16 = bf16[128,1800]{0,1:T(8,128)(2,1)S(1)} fusion(bf16[2,2432,1800]{1,2,0:T(8,128)(2,1)} %param.8, f32[128,2432]{1,0:T(8,128)S(1)} %get-tuple-element.6, f32[128]{0:T(128)S(1)} %add_rsqrt_fusion, f32[128]{0:T(128)S(1)} %broadcast_multiply_fusion), kind=kOutput, calls=%fused_computation.21 | convolution fusion | flops 1121829888 | bytes 10462208 | tf_op jit(solution)/shard_map/dot_general | solution.py:26
  325.7 0.1 reshape.63
  325.8 0.1 slice.62
  325.9 2.2 collective-permute-start
  328.1 0.1 fusion.31
  328.1 10.5 %collective-permute-done = bf16[128,4,300]{0,2,1:T(8,128)(2,1)S(1)} collective-permute-done((bf16[128,4,300]{0,2,1:T(8,128)(2,1)S(1)}, bf16[128,4,300]{0,2,1:T(8,128)(2,1)S(1)}, u32[]{:S(2)}, u32[]{:S(2)}) %collective-permute-start) | collective-permute-done | bytes 307232 | tf_op jit(solution)/shard_map/ppermute | solution.py:15
  338.6 0.3 fusion.54
  338.9 0.1 fusion.32
  339.0 0.3 fusion.21
  339.3 3.4 fusion.8
  (13 shorter events, 0.2 us)
Async XLA Ops:
  6.5 267.2 %all-gather.3.cloned.1.call-start = ((), (), s32[]{:S(2)}) async-start(), calls=%async_computation.1 | async-start | bytes 20234240 | tf_op jit(solution)/shard_map/all_gather | solution.py:48
  147.7 1.1 copy-start
  325.9 12.7 %collective-permute-start = (bf16[128,4,300]{0,2,1:T(8,128)(2,1)S(1)}, bf16[128,4,300]{0,2,1:T(8,128)(2,1)S(1)}, u32[]{:S(2)}, u32[]{:S(2)}) collective-permute-start(bf16[128,4,300]{0,2,1:T(8,128)(2,1)S(1)} %slice.62), channel_id=1, source_target_pairs={{0,1},{1,2},{2,3},{3,4},{4,5},{5,6},{6,7},{7,8},{8,9},{9,10},{10,1... | collective-permute-start | bytes 921608 | tf_op jit(solution)/shard_map/ppermute | solution.py:15
Sparse Core Ops, SparseCore 0:
  156.5 117.1 all-gather.2
where the time goes:
time: 350 us
  waiting for transfers between devices  128 us (37%)
  blocking collectives  115 us (33%)
  local copies, waits for them, and re-layouts  56.2 us (16%)
  matrix products  18.9 us (5%)
  other arithmetic  16.4 us (5%)
  between operations  13.6 us (4%)
    all_gather x1, waiting for transfers between devices, shards(): every_row = lax.all_gather(joined[:, :, HEAD:], 'seq', axis=0, tiled=True)  117 us
    all_gather x1, blocking collectives, shards(): all_codes = lax.all_gather(song_ids, 'seq', axis=0, tiled=True)  83.1 us
    all_to_all x1, blocking collectives, shards(): lax.all_to_all(picked, 'seq', split_axis=0, concat_axis=1, tiled=True)  31.4 us
    reshape x1, local copies, waits for them, and re-layouts, shards(): row_grid = every_row.reshape(axis_count, local_tokens, HEADS, 2 * HEAD)  27.6 us
    gather x2, local copies, waits for them, and re-layouts, shards(): picked = jnp.take(table, all_codes, axis=0)  25 us
    dot_general x2, matrix products, project(): jnp.dot(normalize(residual), weight, preferred_element_type=jnp.float32)  12.3 us
    ppermute x1, waiting for transfers between devices, from_behind(): return lax.ppermute(value, axis, pairs)  10.5 us
    dot_general x1, other arithmetic, shards(): jnp.einsum('chr,rchd->chd', probs, row_grid[..., HEAD:], preferred_elemen...  8.34 us
  transfers between devices with their start and end apart: 2, of which 2 were waited for; matrix products, arithmetic and copies ran while one was open for 0% of the time, Pallas kernels for 0%

commit v1 on v0

--- a/solution.py
+++ b/solution.py
@@ -45,7 +45,9 @@
     residual = embedded.astype(jnp.float32) + position_table.astype(jnp.float32)
     local_tokens = residual.shape[0]
     joined = project(residual, w_qkv[0])
-    every_row = lax.all_gather(joined[:, :, HEAD:], "seq", axis=0, tiled=True)
+    every_row = jnp.concatenate(
+        lax.all_to_all(jnp.stack([joined[:, :, HEAD:]] * lax.axis_size("seq")), "seq", 0, 0), axis=0
+    )
     row_grid = every_row.reshape(axis_count, local_tokens, HEADS, 2 * HEAD)
     scores = (
         jnp.einsum(

time: 350 us -> 501 us (1.43); the launches traced: 350 us -> 494 us
  waiting for transfers between devices: 128 us -> 293 us
  local copies, waits for them, and re-layouts: 56.2 us -> 39.2 us
  between operations: 13.6 us -> 0.22 us
  starting transfers between devices: 2.17 us -> 9.1 us
    all_to_all x0 -> x1, waiting for transfers between devices: none -> 282 us  [shards(): lax.all_to_all(jnp.stack([joined[:, :, HEAD:]] * lax.axis_size('seq')), '...]
    all_gather x1 -> x0, waiting for transfers between devices: 117 us -> none  [shards(): every_row = lax.all_gather(joined[:, :, HEAD:], 'seq', axis=0, tiled=True)]
    reshape x1 -> x0, local copies, waits for them, and re-layouts: 27.6 us -> none  [shards(): row_grid = every_row.reshape(axis_count, local_tokens, HEADS, 2 * HEAD)]
    unnamed x1 -> x3, other arithmetic: 0.02 us -> 18.1 us
    dot_general x2 -> x0, other arithmetic: 15 us -> none  [the longest x1 8.34 us: shards(): jnp.einsum('chr,rchd->chd', probs, row_grid[..., HEAD:], preferred_elemen...]
    another operation x0 -> x1, local copies, waits for them, and re-layouts: none -> 10.9 us  [shards(): jnp.stack([joined[:, :, HEAD:]] * lax.axis_size('seq'))]
    all_to_all x0 -> x1, starting transfers between devices: none -> 7.18 us  [shards(): lax.all_to_all(jnp.stack([joined[:, :, HEAD:]] * lax.axis_size('seq')), '...]
where the time goes in v1:
time: 501 us; the launch traced here: 494 us
  waiting for transfers between devices  293 us (58%)
  blocking collectives  115 us (23%)
  local copies, waits for them, and re-layouts  39.2 us (8%)
  other arithmetic  19.5 us (4%)
  matrix products  19.1 us (4%)
  starting transfers between devices  9.1 us (2%)
    all_to_all x1, waiting for transfers between devices, shards(): lax.all_to_all(jnp.stack([joined[:, :, HEAD:]] * lax.axis_size('seq')), '...  282 us
    all_gather x1, blocking collectives, shards(): all_codes = lax.all_gather(song_ids, 'seq', axis=0, tiled=True)  83.1 us
    all_to_all x1, blocking collectives, shards(): lax.all_to_all(picked, 'seq', split_axis=0, concat_axis=1, tiled=True)  31.4 us
    gather x2, local copies, waits for them, and re-layouts, shards(): picked = jnp.take(table, all_codes, axis=0)  25 us
    unnamed x3, other arithmetic  18.1 us
    dot_general x2, matrix products, project(): jnp.dot(normalize(residual), weight, preferred_element_type=jnp.float32)  12.3 us
    another operation x1, local copies, waits for them, and re-layouts, shards(): jnp.stack([joined[:, :, HEAD:]] * lax.axis_size('seq'))  10.9 us
    ppermute x1, waiting for transfers between devices, from_behind(): return lax.ppermute(value, axis, pairs)  10.7 us
  transfers between devices with their start and end apart: 2, of which 2 were waited for; matrix products, arithmetic and copies ran while one was open for 0% of the time, Pallas kernels for 0%

profile of v1, /device:TPU:32, one launch (start us, length us, event | category | flops | bytes accessed | tf_op | source)
XLA Modules:
  0.0 494.2 jit_solution(4828239279460298627)
XLA Ops:
  0.0 83.1 %all-gather = s32[64,1,128]{2,1,0:T(1,128)S(1)} all-gather(s32[1,1,128]{2,1,0:T(1,128)} %bitcast.78), channel_id=1, replica_groups=mesh['song'=2,'seq'=64] {'seq'}, dimensions={0}, use_global_device_ids=true | all-gather | bytes 33280 | tf_op jit(solution)/shard_map/all_gather | solution.py:42
  83.2 1.2 copy.20
  84.4 24.0 %gather_fusion = bf16[8192,38]{1,0:T(8,128)(2,1)S(1)} fusion(bf16[2048,38]{1,0:T(8,128)(2,1)S(1)} %copy.20, s32[8192]{0:T(1024)S(1)} %fusion.45), kind=kCustom, calls=%fused_computation | custom fusion | bytes 1277952 | tf_op jit(solution)/shard_map/jit(_take)/gather | solution.py:43
  108.4 1.0 copy.21
  109.5 0.1 broadcast_select_fusion
  109.6 31.4 %all_to_all.15 = bf16[64,128,38]{1,2,0:T(8,128)(2,1)S(1)} all-to-all(bf16[64,128,38]{1,2,0:T(8,128)(2,1)S(1)} %broadcast_select_fusion), channel_id=1, replica_groups=mesh['song'=2,'seq'=64] {'seq'}, dimensions={0} | all-to-all | bytes 1245184 | tf_op jit(solution)/shard_map/all_to_all | solution.py:44
  140.9 0.1 convert_bitcast_fusion
  141.0 0.1 reshape.63
  141.1 0.0 copy-start
  141.1 0.4 copy.22
  141.5 0.7 copy-done
  142.2 0.2 fusion.41
  142.4 0.3 multiply_reduce_fusion.3
  142.7 6.2 %fusion.13 = bf16[128,1800]{0,1:T(8,128)(2,1)S(1)} fusion(bf16[2,2432,1800]{1,2,0:T(8,128)(2,1)} %param.8, f32[128]{0:T(128)S(1)} %add_rsqrt_fusion.1, f32[128]{0:T(128)S(1)} %broadcast_multiply_fusion.1, f32[128,2432]{1,0:T(8,128)S(1)} %copy.22, bf16[128,2432]{1,0:T(8,128)(2,1)S(1)} %copy-done), kind=kOutput, calls=%fused_computation.20 | convolution fusion | flops 1122452480 | bytes 11084800 | tf_op jit(solution)/shard_map/dot_general | solution.py:26
  148.9 0.1 reshape.59
  149.1 0.1 slice.59
  149.2 0.1 copy.23
  149.3 10.9 %stack.2 = bf16[64,128,4,300]{1,2,3,0:T(4,128)(2,1)} broadcast(bf16[128,4,300]{0,1,2:T(4,128)(2,1)S(1)} %copy.23), dimensions={1,2,3} | broadcast | bytes 19968000 | tf_op jit(solution)/shard_map/stack | solution.py:49
  160.2 7.2 %all-to-all-start.1 = ((bf16[64,128,4,300]{1,2,3,0:T(4,128)(2,1)}), bf16[64,128,4,300]{1,2,3,0:T(4,128)(2,1)}, u32[]{:S(2)}, u32[]{:S(2)}) async-start(bf16[64,128,4,300]{1,2,3,0:T(4,128)(2,1)} %stack.2), calls=%async_computation.1 | async-start | bytes 39321600 | tf_op jit(solution)/shard_map/all_to_all | solution.py:49
  167.4 0.1 copy.47
  167.5 281.9 %all-to-all-done.1 = bf16[64,128,4,300]{1,2,3,0:T(4,128)(2,1)} async-done(((bf16[64,128,4,300]{1,2,3,0:T(4,128)(2,1)}), bf16[64,128,4,300]{1,2,3,0:T(4,128)(2,1)}, u32[]{:S(2)}, u32[]{:S(2)}) %all-to-all-start.1) | async-done | bytes 19660832 | tf_op jit(solution)/shard_map/all_to_all | solution.py:49
  449.5 9.0 %multiply_reduce_fusion.1 = f32[128,4,64]{0,1,2:T(4,128)S(1)} fusion(bf16[64,128,4,300]{1,2,3,0:T(4,128)(2,1)} %all-to-all-done.1, f32[128,4,150]{0,1,2:T(4,128)S(1)} %copy.47), kind=kLoop, calls=%fused_computation.4 | loop fusion | flops 14712832 | bytes 10268672
  458.5 0.1 fusion.26
  458.6 0.1 copy.48
  458.7 9.1 %multiply_reduce_fusion = bf16[128,4,150]{0,1,2:T(4,128)(2,1)S(1)} fusion(bf16[64,128,4,300]{1,2,3,0:T(4,128)(2,1)} %all-to-all-done.1, f32[128,4,64]{0,1,2:T(4,128)S(1)} %copy.48), kind=kLoop, calls=%fused_computation.3 | loop fusion | flops 14668800 | bytes 10115072
  467.9 2.8 fusion.57
  470.7 0.3 multiply_reduce_fusion.2
  471.0 6.2 %fusion.16 = bf16[128,1800]{0,1:T(8,128)(2,1)S(1)} fusion(bf16[2,2432,1800]{1,2,0:T(8,128)(2,1)} %param.8, f32[128,2432]{1,0:T(8,128)S(1)} %get-tuple-element.6, f32[128]{0:T(128)S(1)} %add_rsqrt_fusion, f32[128]{0:T(128)S(1)} %broadcast_multiply_fusion), kind=kOutput, calls=%fused_computation.21 | convolution fusion | flops 1121829888 | bytes 10462208 | tf_op jit(solution)/shard_map/dot_general | solution.py:26
  477.2 0.1 reshape.61
  477.3 0.1 slice.62
  477.4 1.9 collective-permute-start
  479.3 0.1 fusion.31
  479.4 10.7 %collective-permute-done = bf16[128,4,300]{0,2,1:T(8,128)(2,1)S(1)} collective-permute-done((bf16[128,4,300]{0,2,1:T(8,128)(2,1)S(1)}, bf16[128,4,300]{0,2,1:T(8,128)(2,1)S(1)}, u32[]{:S(2)}, u32[]{:S(2)}) %collective-permute-start) | collective-permute-done | bytes 307232 | tf_op jit(solution)/shard_map/ppermute | solution.py:15
  490.1 0.3 fusion.58
  490.4 0.1 fusion.32
  490.5 0.3 fusion.21
  490.9 3.4 fusion.8
  (14 shorter events, 0.2 us)
Async XLA Ops:
  141.1 1.1 copy-start
  160.2 289.3 %all-to-all-start.1 = ((bf16[64,128,4,300]{1,2,3,0:T(4,128)(2,1)}), bf16[64,128,4,300]{1,2,3,0:T(4,128)(2,1)}, u32[]{:S(2)}, u32[]{:S(2)}) async-start(bf16[64,128,4,300]{1,2,3,0:T(4,128)(2,1)} %stack.2), calls=%async_computation.1 | async-start | bytes 39321600 | tf_op jit(solution)/shard_map/all_to_all | solution.py:49
  477.4 12.7 %collective-permute-start = (bf16[128,4,300]{0,2,1:T(8,128)(2,1)S(1)}, bf16[128,4,300]{0,2,1:T(8,128)(2,1)S(1)}, u32[]{:S(2)}, u32[]{:S(2)}) collective-permute-start(bf16[128,4,300]{0,2,1:T(8,128)(2,1)S(1)} %slice.62), channel_id=1, source_target_pairs={{0,1},{1,2},{2,3},{3,4},{4,5},{5,6},{6,7},{7,8},{8,9},{9,10},{10,1... | collective-permute-start | bytes 921608 | tf_op jit(solution)/shard_map/ppermute | solution.py:15
